TPU v7x, 32 devices: a whole 2x2x4 slice. The times are simulated.
32 devices in a mesh: guide: 2 (over core), tensor: 2 (over y), batch: 8 (over z, x).
Axes of the slice: x: 2, y: 2, z: 4, core: 2. Of those that a mesh axis runs over, the one named last changes fastest.
Arguments:
- latents: float32 [8, 16, 448], P('batch'), may hold values from -6 to 6
- lengths: int32 [8], P('batch'), may hold values from 1 to 448, 2240 in all
- timesteps: int32 [8], P('batch'), may hold values from 100 to 599
- guidance: float32 [8], P('batch'), may hold values from 1.5 to 6
- condition: float32 [2, 8, 1152], P('guide', 'batch'), may hold values from -6 to 6
- embed_weight: float32 [16, 1152], replicated, may hold values from -1.5 to 1.5
- modulation_weight: bfloat16 [2, 1152, 6, 1152], P(None, 'batch', None, 'tensor'), may hold values from -0.1875 to 0.1875
- final_modulation: bfloat16 [1152, 2, 1152], P('batch', None, 'tensor'), may hold values from -0.1875 to 0.1875
- qkv_weight: bfloat16 [2, 1152, 3, 1152], P(None, 'batch', None, 'tensor'), may hold values from -15 to 15
- proj_weight: bfloat16 [2, 1152, 1152], P(None, 'tensor', 'batch'), may hold values from -0.1875 to 0.1875
- up_weight: bfloat16 [2, 1152, 4608], P(None, 'batch', 'tensor'), may hold values from -0.1875 to 0.1875
- down_weight: bfloat16 [2, 4608, 1152], P(None, 'tensor', 'batch'), may hold values from -0.09375 to 0.09375
- output_weight: bfloat16 [1152, 16], replicated, may hold values from -0.1875 to 0.1875
Outputs:
- guided_noise: float32 [8, 16, 448], P('batch', 'guide', 'tensor')
- previous_latents: float32 [8, 16, 448], P('batch', 'guide', 'tensor')
Inputs may be any that keep to these rules, and one draw needn't show every extreme that they name: `lengths`: at least one request has exactly 448 live tokens; all requests together have 8 * 448 * 5 // 8.
All inputs are finite; a program needn't handle non-finite values. No bound on the sum of `lengths` on one device may be relied on, other than what follows from the above.
Results may differ from a plain program's by a relative error of at most 0.025.
Values may be sent and summed in bfloat16 or wider, within the bound.
No kernel may reach another device: no remote copies, remote signals or barrier semaphores. Data moves between devices by JAX's collectives and lax.ppermute only.
A program may use at most 128 MiB of HBM per device.

v0:
```python
import functools
import math

import jax
import jax.numpy as jnp
import numpy as np
from jax import lax
from jax.experimental import pallas as pl
from jax.experimental.pallas import tpu as pltpu
from jax.sharding import PartitionSpec as P

HDIM = 72
TRAIN_STEPS = 1000
STRIDE = 20


norm_epsilon = 1e-06


def from_partner(block, axis, distance):
    count = lax.axis_size(axis)
    route = []
    for low in range(count):
        high = low | 1 << distance
        if high != low and high < count:
            route += [(low, high), (high, low)]
    return lax.ppermute(block, axis, route)


def layer_norm(values):
    center = values - jnp.mean(values, axis=-1, keepdims=True)
    spread = jnp.mean(center * center, axis=-1, keepdims=True)
    return center * lax.rsqrt(spread + norm_epsilon)


def modulate(values, shift, scale):
    return layer_norm(values) * (1.0 + scale[:, None, :]) + shift[:, None, :]


def position_table(row_count, width):
    rows_at = jnp.arange(row_count, dtype=jnp.int32).astype(jnp.float32)
    half_width = width // 2
    frequency = jnp.exp(
        jnp.arange(half_width, dtype=jnp.float32) * (-math.log(10000.0) / half_width)
    )
    angles = rows_at[:, None] * frequency[None, :]
    return jnp.concatenate([jnp.sin(angles), jnp.cos(angles)], axis=1)


def attend(operands):
    projected_item, key_live = operands
    score_scale = 1.0 / math.sqrt(HDIM)
    scores = (
        jnp.einsum(
            "qhd,khd->hqk",
            projected_item[:, 0],
            projected_item[:, 1],
            preferred_element_type=jnp.float32,
        )
        * score_scale
    )
    scores = jnp.where(key_live[None, None, :], scores, -jnp.inf)
    row_max = jnp.max(scores, axis=-1, keepdims=True)
    exp_scores = jnp.exp(scores - row_max)
    probabilities = (exp_scores / jnp.sum(exp_scores, axis=-1, keepdims=True)).astype(jnp.bfloat16)
    attended = jnp.einsum(
        "hqk,khd->qhd", probabilities, projected_item[:, 2], preferred_element_type=jnp.float32
    )
    return attended.astype(jnp.bfloat16).reshape(
        attended.shape[0], attended.shape[1] * attended.shape[2]
    )


def local(
    latents,
    lengths,
    timesteps,
    guidance,
    condition,
    embed_weight,
    modulation_weight,
    final_modulation,
    qkv_weight,
    proj_weight,
    up_weight,
    down_weight,
    output_weight,
):
    tensor_count = lax.axis_size("tensor")
    batch_count = lax.axis_size("batch")
    tensor_at = lax.axis_index("tensor")
    batch_at = lax.axis_index("batch")
    req_local, patch_size, max_len = latents.shape
    width = embed_weight.shape[1]
    layer_count = qkv_weight.shape[0]
    head_cols = qkv_weight.shape[3]
    heads_local = head_cols // HDIM
    rows_local = max_len // tensor_count
    width_piece = width // batch_count
    mod_count = 6 * layer_count + 2

    def rows_product(activation, shard):
        return jnp.dot(
            activation,
            lax.all_gather(shard, "batch", axis=0, tiled=True),
            preferred_element_type=jnp.float32,
        )

    def cols_product(activation, shard):
        return jnp.dot(
            activation,
            lax.all_gather(shard, "batch", axis=1, tiled=True),
            preferred_element_type=jnp.float32,
        )

    cond_act = jax.nn.silu(condition[0]).astype(jnp.bfloat16)
    cond_all = lax.all_gather(cond_act, "batch", axis=0, tiled=True)
    cond_cols = lax.dynamic_slice_in_dim(cond_all, batch_at * width_piece, width_piece, 1)
    block_local = jnp.transpose(modulation_weight, (1, 0, 2, 3)).reshape(
        width_piece, 6 * layer_count * head_cols
    )
    mod_local = jnp.concatenate(
        [block_local, final_modulation.reshape(width_piece, 2 * head_cols)], axis=1
    )
    mod_mine = lax.psum_scatter(
        jnp.dot(cond_cols, mod_local, preferred_element_type=jnp.float32),
        "batch",
        scatter_dimension=0,
        tiled=True,
    )
    mod_full = lax.all_gather(
        mod_mine.reshape(req_local, mod_count, head_cols), "tensor", axis=2, tiled=True
    )
    positions = jnp.arange(max_len, dtype=jnp.int32)
    live_mask = positions[None, :] < lengths[:, None]
    own_start = tensor_at * rows_local
    hidden_state = (
        jnp.einsum("rpl,pd->rld", latents, embed_weight, precision=lax.Precision.HIGHEST)
        + position_table(max_len, width)[None]
    )
    for layer_at in range(layer_count):
        modulation = mod_full[:, 6 * layer_at : 6 * layer_at + 6]
        normed = modulate(hidden_state, modulation[:, 0], modulation[:, 1]).astype(jnp.bfloat16)
        projected = rows_product(
            normed.reshape(req_local * max_len, width),
            qkv_weight[layer_at].reshape(width_piece, 3 * head_cols),
        ).astype(jnp.bfloat16)
        projected = projected.reshape(req_local, max_len, 3, heads_local, HDIM)
        attended = lax.map(attend, (projected, live_mask))
        branch = cols_product(
            attended.reshape(req_local * max_len, head_cols), proj_weight[layer_at]
        ).reshape(req_local, max_len, width)
        branch = lax.psum(branch.astype(jnp.bfloat16), "tensor").astype(jnp.float32)
        hidden_state = hidden_state + modulation[:, 2][:, None, :] * branch
        normed = modulate(hidden_state, modulation[:, 3], modulation[:, 4]).astype(jnp.bfloat16)
        hidden_units = jax.nn.gelu(
            rows_product(normed.reshape(req_local * max_len, width), up_weight[layer_at]),
            approximate=True,
        ).astype(jnp.bfloat16)
        branch = cols_product(hidden_units, down_weight[layer_at]).reshape(
            req_local, max_len, width
        )
        branch = lax.psum(branch.astype(jnp.bfloat16), "tensor").astype(jnp.float32)
        hidden_state = hidden_state + modulation[:, 5][:, None, :] * branch
    hidden_state = lax.dynamic_slice_in_dim(hidden_state, own_start, rows_local, 1)
    final_in = modulate(
        hidden_state, mod_full[:, 6 * layer_count], mod_full[:, 6 * layer_count + 1]
    ).astype(jnp.bfloat16)
    noise_own = jnp.einsum(
        "rld,dp->rpl", final_in, output_weight, preferred_element_type=jnp.float32
    )
    return finish(latents, lengths, timesteps, guidance, noise_own, rows_local)


def alpha_table():
    beta_values = np.linspace(0.0001, 0.02, TRAIN_STEPS, dtype=np.float32)
    return np.cumprod(np.float32(1.0) - beta_values, dtype=np.float32)


def finish(latents, lengths, timesteps, guidance, noise_own, rows_local):
    patch_size, max_len = latents.shape[1:]
    guide_at = lax.axis_index("guide")
    is_first = guide_at == 0
    own_start = lax.axis_index("tensor") * rows_local
    own_latents = lax.dynamic_slice_in_dim(latents, own_start, rows_local, 2)
    own_live = (own_start + jnp.arange(rows_local, dtype=jnp.int32))[None, :] < lengths[:, None]
    half_patch = patch_size // 2
    mine_noise = lax.dynamic_slice_in_dim(noise_own, guide_at * half_patch, half_patch, 1)
    other_noise = lax.dynamic_slice_in_dim(noise_own, (1 - guide_at) * half_patch, half_patch, 1)
    partner_noise = from_partner(other_noise, "guide", 0)
    cond_noise = jnp.where(is_first, mine_noise, partner_noise)
    uncond_noise = jnp.where(is_first, partner_noise, mine_noise)
    live_out = own_live[:, None, :]
    guided = uncond_noise + guidance[:, None, None] * (cond_noise - uncond_noise)
    guided = jnp.where(live_out, guided, 0.0)
    half_latents = lax.dynamic_slice_in_dim(own_latents, guide_at * half_patch, half_patch, 1)
    alpha_bar = jnp.asarray(alpha_table())
    step_ids = jnp.arange(TRAIN_STEPS, dtype=jnp.int32)
    alpha_now = jnp.sum(
        jnp.where(step_ids[None, :] == timesteps[:, None], alpha_bar[None, :], 0.0), axis=1
    )[:, None, None]
    alpha_prev = jnp.sum(
        jnp.where(step_ids[None, :] == (timesteps - STRIDE)[:, None], alpha_bar[None, :], 0.0),
        axis=1,
    )[:, None, None]
    start_est = (half_latents - jnp.sqrt(1.0 - alpha_now) * guided) / jnp.sqrt(alpha_now)
    previous = jnp.sqrt(alpha_prev) * start_est + jnp.sqrt(1.0 - alpha_prev) * guided
    previous = jnp.where(live_out, previous, 0.0)
    return (guided, previous)


def exchange(block, axis, bit):
    count = lax.axis_size(axis)
    return lax.ppermute(block, axis, [(at, at ^ bit) for at in range(count)])


def after(value, *earlier):
    return lax.optimization_barrier((value, *earlier))[0]


HOLDS = {"own": (0,), "two": (4,), "pair": (0, 4), "four": (2, 6)}

PLAN = (
    ((("own", 0),), (("own", 0),)),
    ((("pair", 0),), (("two", 0), ("own", 1))),
    ((("own", 1),), (("four", 0),)),
    ((("pair", 1), ("own", 2)), (("two", 1), ("own", 2), ("own", 3))),
    ((("pair", 2), ("own", 3)), (("four", 1), ("two", 2))),
    ((("pair", 3), ("own", 4)), (("four", 2), ("two", 3))),
    ((("pair", 4), ("own", 5)), (("four", 3), ("pair", 4))),
    ((("pair", 5),), (("four", 4), ("pair", 5))),
    ((), (("four", 5),)),
)
READY = ((0,), (1, 2), (3,), (), (4, 5))


class Stream:
    def __init__(self, make_own):
        self.make_own, self.at, self.last = make_own, 0, None
        self.values, self.arrived, self.sent = {}, {}, ()
        self.blocks = [[] for _ in make_own]

    def hand_over(self, array, parts, flip, anchor):
        earlier = []
        other = self.last = exchange(after(array, *earlier) if earlier else array, "guide", 1)
        at = 0
        for kind, piece in parts:
            for distance in HOLDS[kind]:
                for which, buffer in enumerate((array, other)):
                    self.blocks[piece].append((buffer, at, distance ^ flip, which))
                at += 1

    def step(self, *first):
        over_z, over_x = PLAN[self.at] if self.at < len(PLAN) else ((), ())
        for piece in READY[self.at] if self.at < len(READY) else ():
            self.values["own", piece] = self.make_own[piece]()
        self.at += 1
        self.values, arrived, _ = lax.optimization_barrier((self.values, self.arrived, first))
        self.values = values = dict(self.values)
        for (kind, piece), value in arrived.items():
            if kind == "own":
                values["two", piece] = value
                values["pair", piece] = jnp.concatenate([values["own", piece], value], axis=0)
            elif kind == "pair":
                values["four", piece] = value
        came = arrived.get("x")
        self.arrived, anchor = {}, None
        source = [values[part] for part in over_x]
        if source:
            source = source[0] if len(source) == 1 else jnp.concatenate(source, axis=0)
            self.arrived["x", ""] = exchange(source, "batch", 1)
        for kind, piece in over_z:
            sent = exchange(values[kind, piece], "batch", 4 if kind == "own" else 2)
            self.arrived[kind, piece] = sent
            anchor = sent if anchor is None else anchor
        if ("x", "") in arrived:
            self.hand_over(arrived["x", ""], self.sent, 1, None)
        if over_x:
            self.hand_over(source, over_x, 0, anchor)
        self.sent = over_x

    def operands(self, piece):
        arrays, places = [], []
        for buffer, at, distance, which in self.blocks[piece]:
            found = [n for n, array in enumerate(arrays) if array is buffer]
            if not found:
                arrays.append(buffer)
            places.append((found[0] if found else len(arrays) - 1, at, distance, which))
        return arrays, places


def fetch(weights, slots, buffers, places, batch_at, arrivals):
    rows = weights.shape[1] // (len(places) // 2)
    copies = []
    for number, (array, at, distance, which) in enumerate(places):
        row = pl.multiple_of((batch_at ^ distance) * rows, 16)
        copies.append(
            pltpu.make_async_copy(
                buffers[array].at[pl.ds(at * rows, rows), :],
                weights.at[slots[which], pl.ds(row, rows), :],
                arrivals.at[number],
            )
        )
        copies[-1].start()
    return copies


def normalized(hidden, shift, scale):
    center = hidden - jnp.mean(hidden, axis=-1, keepdims=True)
    spread = jnp.mean(center * center, axis=-1, keepdims=True)
    return center * lax.rsqrt(spread + norm_epsilon) * (1.0 + scale) + shift


def dot_nt(left, right):
    return lax.dot_general(
        left, right, (((1,), (1,)), ((), ())), preferred_element_type=jnp.float32
    )


def kernel_call(body, outs, scratch, operands, buffers, flops, bytes_moved):
    specs = [pl.BlockSpec(memory_space=pltpu.SMEM)]
    specs += [pl.BlockSpec(memory_space=pltpu.VMEM) for _ in operands[1:]]
    specs += [pl.BlockSpec(memory_space=pl.ANY) for _ in buffers]
    if buffers:
        scratch = scratch + [pltpu.SemaphoreType.DMA((16,))]
    return pl.pallas_call(
        body,
        out_shape=outs,
        in_specs=specs,
        out_specs=jax.tree.map(lambda _: pl.BlockSpec(memory_space=pltpu.VMEM), outs),
        scratch_shapes=scratch,
        cost_estimate=pl.CostEstimate(
            flops=int(flops), bytes_accessed=int(bytes_moved), transcendentals=0
        ),
        compiler_params=pltpu.CompilerParams(vmem_limit_bytes=44 * 2**20),
    )(*operands, *buffers)


def enter(hidden, branches, mods, row, hidden_out, normed):
    state = hidden[...]
    if branches:
        total = branches[0][...].astype(jnp.float32) + branches[1][...].astype(jnp.float32)
        state = state + mods[row - 1 : row, :] * total
        hidden_out[...] = state
    normed[...] = normalized(state, mods[row : row + 1, :], mods[row + 1 : row + 2, :]).astype(
        jnp.bfloat16
    )


def qkv_kernel(places, array_count, layer, heads, branch_count, ids, hidden, mods, *refs):
    branches, refs = refs[:branch_count], refs[branch_count:]
    buffers, refs = refs[:array_count], refs[array_count:]
    hidden_out = None
    if branches:
        hidden_out, refs = refs[0], refs[1:]
    heads_out, proj_out, weights, normed, projected, arrivals = refs
    width = hidden.shape[1]
    half = width // 2
    copies = fetch(weights, [ids[1], 1 - ids[1]], buffers, places, ids[0], arrivals)
    enter(hidden, branches, mods, 6 * layer, hidden_out, normed)
    for copy in copies:
        copy.wait()
    proj_out[...] = weights[1, :, half:]

    def step(at, carry):
        lo = pl.multiple_of(at * 384, 128)
        projected[:, pl.ds(lo, 384)] = jnp.dot(
            normed[...], weights[0, :, pl.ds(lo, 384)], preferred_element_type=jnp.float32
        ).astype(jnp.bfloat16)
        return carry

    lax.fori_loop(0, width // 384, step, 0)
    projected[:, width:] = jnp.dot(
        normed[...], weights[1, :, :half], preferred_element_type=jnp.float32
    ).astype(jnp.bfloat16)
    for at in range(3 * heads):
        heads_out[at] = projected[:, at * HDIM : (at + 1) * HDIM]


def attention_kernel(heads, ids, heads_in, proj, partial, attended):
    keys = heads_in.shape[1]
    factor = math.log2(math.e) / math.sqrt(HDIM)
    live = lax.broadcasted_iota(jnp.int32, (1, keys), 1) < ids[3]
    for at in range(heads):
        scores = dot_nt(heads_in[at], heads_in[heads + at])
        scores = jnp.where(live, scores * factor, -jnp.inf)
        raised = jnp.exp2(scores - jnp.max(scores, axis=-1, keepdims=True))
        total = jnp.sum(raised, axis=-1, keepdims=True)
        out = jnp.dot(
            raised.astype(jnp.bfloat16), heads_in[2 * heads + at], preferred_element_type=jnp.float32
        )
        attended[:, at * HDIM : (at + 1) * HDIM] = (out / total).astype(jnp.bfloat16)
    partial[...] = dot_nt(attended[...], proj[...]).astype(jnp.bfloat16)


def up_kernel(places, array_count, layer, ids, hidden, mods, *refs):
    branches, refs = refs[:2], refs[2:]
    buffers, refs = refs[:array_count], refs[array_count:]
    hidden_out, units, weights, normed, arrivals = refs
    width = hidden.shape[1]
    copies = fetch(weights, [0, 1], buffers, places, ids[0], arrivals)
    enter(hidden, branches, mods, 6 * layer + 3, hidden_out, normed)
    for copy in copies:
        copy.wait()
    for half in range(2):

        def step(at, carry):
            lo = pl.multiple_of(at * 384, 128)
            product = jnp.dot(
                normed[...], weights[half, :, pl.ds(lo, 384)], preferred_element_type=jnp.float32
            )
            inner = math.sqrt(2.0 / math.pi) * (product + 0.044715 * product * product * product)
            units[half, :, pl.ds(lo, 384)] = (0.5 * product * (1.0 + jnp.tanh(inner))).astype(
                jnp.bfloat16
            )
            return carry

        lax.fori_loop(0, width // 384, step, 0)


def down_kernel(places, array_count, ids, units, *refs):
    buffers, (partial, weights, arrivals) = refs[:array_count], refs[array_count:]
    width = partial.shape[1]
    for copy in fetch(weights, [0, 1], buffers, places, ids[0], arrivals):
        copy.wait()

    def step(at, carry):
        lo = pl.multiple_of(at * 384, 128)
        product = dot_nt(units[0], weights[0, pl.ds(lo, 384), :])
        product = product + dot_nt(units[1], weights[1, pl.ds(lo, 384), :])
        partial[:, pl.ds(lo, 384)] = product.astype(jnp.bfloat16)
        return carry

    lax.fori_loop(0, width // 384, step, 0)


def modulation_sums(columns, modulation_weight, final_modulation):
    layer_count, _, _, head_cols = modulation_weight.shape
    blocks = jnp.einsum(
        "rk,lkjc->rljc", columns, modulation_weight, preferred_element_type=jnp.float32
    ).reshape(columns.shape[0], 6 * layer_count, head_cols)
    finals = jnp.einsum("rk,kjc->rjc", columns, final_modulation, preferred_element_type=jnp.float32)
    return jnp.concatenate([blocks, finals], axis=1)


def all_columns(mine):
    other = exchange(mine, "tensor", 1)
    first = lax.axis_index("tensor") == 0
    return jnp.concatenate(
        [jnp.where(first, mine, other), jnp.where(first, other, mine)], axis=1
    )


def fast_local(
    latents,
    lengths,
    timesteps,
    guidance,
    condition,
    embed_weight,
    modulation_weight,
    final_modulation,
    qkv_weight,
    proj_weight,
    up_weight,
    down_weight,
    output_weight,
):
    tensor_at = lax.axis_index("tensor")
    batch_at = lax.axis_index("batch")
    guide_at = lax.axis_index("guide")
    _, patch_size, max_len = latents.shape
    width = embed_weight.shape[1]
    half = width // 2
    layer_count = qkv_weight.shape[0]
    heads = half // HDIM
    rows_own = max_len // 2
    width_piece = qkv_weight.shape[1]
    first = guide_at == 0
    ids = jnp.stack([batch_at, guide_at, tensor_at, lengths[0]]).astype(jnp.int32)
    bf16, f32 = jnp.bfloat16, jnp.float32

    def attention_piece(layer):
        queries_keys = qkv_weight[layer, :, :2].reshape(width_piece, width)
        values_proj = jnp.concatenate([qkv_weight[layer, :, 2], proj_weight[layer].T], axis=1)
        return jnp.where(first, queries_keys, values_proj)

    def up_piece(layer):
        return lax.dynamic_slice_in_dim(up_weight[layer], guide_at * width, width, 1)

    def down_piece(layer):
        return lax.dynamic_slice_in_dim(down_weight[layer], guide_at * width, width, 0).T

    stream = Stream(
        [
            functools.partial(make, layer)
            for layer in range(layer_count)
            for make in (attention_piece, up_piece, down_piece)
        ]
    )
    weight_bytes = 4 * width * width
    shape = jax.ShapeDtypeStruct
    two_weights = pltpu.VMEM((2, width, width), bf16)
    normed = pltpu.VMEM((max_len, width), bf16)

    def attention_block(layer, hidden, mods, branches):
        outs = [shape((3 * heads, max_len, HDIM), bf16), shape((width, half), bf16)]
        if branches:
            outs = [shape((max_len, width), f32)] + outs
        arrays, places = stream.operands(3 * layer)
        results = kernel_call(
            functools.partial(qkv_kernel, places, len(arrays), layer, heads, len(branches)),
            outs,
            [two_weights, normed, pltpu.VMEM((max_len, 3 * half), bf16)],
            [ids, hidden, mods, *branches],
            arrays,
            2 * max_len * width * 3 * half,
            weight_bytes,
        )
        partial = kernel_call(
            functools.partial(attention_kernel, heads),
            shape((max_len, width), bf16),
            [pltpu.VMEM((max_len, half), bf16)],
            [ids, *results[-2:]],
            [],
            4 * max_len * max_len * half + 2 * max_len * half * width,
            weight_bytes,
        )
        return results[0] if branches else hidden, partial

    def both(partial):
        return [partial, exchange(partial, "tensor", 1)]

    def up_block(layer, hidden, mods, branches):
        arrays, places = stream.operands(3 * layer + 1)
        return kernel_call(
            functools.partial(up_kernel, places, len(arrays), layer),
            [shape((max_len, width), f32), shape((2, max_len, width), bf16)],
            [two_weights, normed],
            [ids, hidden, mods, *branches],
            arrays,
            4 * max_len * width * width,
            weight_bytes,
        )

    def down_block(layer, units):
        arrays, places = stream.operands(3 * layer + 2)
        return kernel_call(
            functools.partial(down_kernel, places, len(arrays)),
            shape((max_len, width), bf16),
            [two_weights],
            [ids, units],
            arrays,
            4 * max_len * width * width,
            weight_bytes,
        )

    activated = jax.nn.silu(condition[0]).astype(bf16).reshape(-1, width_piece)
    stream.step()
    columns = lax.all_to_all(activated, "batch", 0, 0, tiled=True)
    stream.step(columns)
    sums = modulation_sums(columns, modulation_weight, final_modulation)
    mine = jnp.sum(lax.all_to_all(sums, "batch", 0, 0, tiled=True), axis=0)
    stream.step()
    hidden = jnp.einsum(
        "pl,pd->ld", latents[0], embed_weight, precision=lax.Precision.HIGHEST
    ) + position_table(max_len, width)
    stream.step(mine, hidden)
    mods = all_columns(mine)
    hidden, partial = attention_block(0, hidden, mods, [])
    stream.step(partial)
    branches = both(partial)
    stream.step(branches)
    hidden, units = up_block(0, hidden, mods, branches)
    stream.step(units)
    partial = down_block(0, units)
    stream.step(partial)
    hidden, partial = attention_block(1, hidden, mods, both(partial))
    stream.step(partial)
    branches = both(partial)
    stream.step()
    hidden, units = up_block(1, hidden, mods, branches)
    partial = down_block(1, units)
    own_start = tensor_at * rows_own
    mine = lax.dynamic_slice_in_dim(partial, own_start, rows_own, 0)
    theirs = exchange(
        lax.dynamic_slice_in_dim(partial, (1 - tensor_at) * rows_own, rows_own, 0), "tensor", 1
    )
    hidden = lax.dynamic_slice_in_dim(hidden, own_start, rows_own, 0)
    hidden = hidden + mods[6 * layer_count - 1][None, :] * (
        mine.astype(f32) + theirs.astype(f32)
    )
    final_in = normalized(
        hidden, mods[6 * layer_count][None, :], mods[6 * layer_count + 1][None, :]
    ).astype(bf16)
    noise_own = lax.dot_general(
        output_weight, final_in, (((0,), (1,)), ((), ())), preferred_element_type=f32
    )[None]
    return finish(latents, lengths, timesteps, guidance, noise_own, rows_own)


def solution(mesh):
    in_specs = (
        P("batch", None, None),
        P("batch"),
        P("batch"),
        P("batch"),
        P("guide", "batch", None),
        P(),
        P(None, "batch", None, "tensor"),
        P("batch", None, "tensor"),
        P(None, "batch", None, "tensor"),
        P(None, "tensor", "batch"),
        P(None, "batch", "tensor"),
        P(None, "tensor", "batch"),
        P(),
    )
    out_specs = (P("batch", "guide", "tensor"), P("batch", "guide", "tensor"))
    sizes = mesh.shape
    small = sizes["batch"] == 8 and sizes["tensor"] == 2
    body = fast_local if small else local
    return jax.shard_map(body, mesh=mesh, in_specs=in_specs, out_specs=out_specs, check_vma=False)
```

profile of v0, /device:TPU:1, one launch (start us, length us, event | category | flops | bytes accessed | tf_op | source)
XLA Modules:
  0.0 317.8 jit_solution(17254313043622171035)
XLA Ops:
  7.0 3.8 %collective-permute-start.2 = (bf16[144,1152]{1,0:T(8,128)(2,1)S(1)}, bf16[144,1152]{1,0:T(8,128)(2,1)}, u32[]{:S(2)}, u32[]{:S(2)}) collective-permute-start(bf16[144,1152]{1,0:T(8,128)(2,1)S(1)} %maximum_select_fusion.refs_0_), channel_id=1, source_target_pairs={{0,4},{1,5},{2,6},{3,7},{4,0},{5,1},{6,2},{7,3},{8,12},{9,13},{10,... | collective-permute-start | bytes 995336 | tf_op jit(solution)/shard_map/ppermute | solution.py:214
  12.7 3.3 %all-to-all-start = ((bf16[8,1,144]{2,1,0:T(2,128)(2,1)}), bf16[8,1,144]{2,1,0:T(2,128)(2,1)S(1)}, u32[]{:S(2)}, u32[]{:S(2)}) async-start(bf16[8,1,144]{2,1,0:T(2,128)(2,1)} %copy.27), calls=%async_computation | async-start | bytes 16384 | tf_op jit(solution)/shard_map/all_to_all | solution.py:560
  35.1 5.8 %multiply_sine_fusion = (f32[448,576]{1,0:T(8,128)}, f32[448,576]{1,0:T(8,128)}) fusion(f32[576]{0:T(1024)S(1)} %multiply_exponential_fusion, f32[448]{0:T(512)S(1)} %iota_convert_fusion), kind=kLoop, calls=%fused_computation.2 | loop fusion | flops 258048 | bytes 2068480 | tf_op jit(solution)/shard_map/sin | solution.py:47
  41.3 5.5 %collective-permute-done.6.refs_8_ = bf16[288,1152]{1,0:T(8,128)(2,1)S(1)} collective-permute-done((bf16[288,1152]{1,0:T(8,128)(2,1)}, bf16[288,1152]{1,0:T(8,128)(2,1)S(1)}, u32[]{:S(2)}, u32[]{:S(2)}) %collective-permute-start.6) | collective-permute-done | bytes 663584 | tf_op jit(solution)/shard_map/ppermute | solution.py:214
  51.5 4.2 %all-to-all-start.1 = ((f32[8,14,576]{2,1,0:T(8,128)}), f32[8,14,576]{2,1,0:T(8,128)}, u32[]{:S(2)}, u32[]{:S(2)}) async-start(f32[8,14,576]{2,1,0:T(8,128)} %copy.29), calls=%async_computation.1 | async-start | bytes 655360 | tf_op jit(solution)/shard_map/all_to_all | solution.py:563
  59.3 3.4 %convolution_add_fusion.hidden = f32[448,1152]{1,0:T(8,128)S(1)} fusion(f32[16,1152]{1,0:T(8,128)S(1)} %copy-done.39, f32[448,576]{1,0:T(8,128)} %get-tuple-element.138, f32[448,576]{1,0:T(8,128)} %get-tuple-element.137, f32[1,16,448]{2,1,0:T(8,128)S(1)} %copy-done.40), kind=kOutput, calls=%fused_computation | convolution fusion | flops 100122624 | bytes 4231168 | tf_op jit(solution)/shard_map/pl,pd->ld/dot_general | solution.py:565
  62.7 3.1 collective-permute-start.5
  67.4 11.3 %collective-permute-done.10 = bf16[144,1152]{1,0:T(8,128)(2,1)} collective-permute-done((bf16[144,1152]{1,0:T(8,128)(2,1)}, bf16[144,1152]{1,0:T(8,128)(2,1)}, u32[]{:S(2)}, u32[]{:S(2)}) %collective-permute-start.10) | collective-permute-done | bytes 331808 | tf_op jit(solution)/shard_map/ppermute | solution.py:214
  92.3 8.5 %shard_map.149 = (bf16[24,448,72]{2,1,0:T(8,128)(2,1)}, bf16[1152,576]{1,0:T(8,128)(2,1)S(1)}) custom-call(s32[4]{0:T(128)S(1)} %pad_add_fusion.ids, f32[448,1152]{1,0:T(8,128)S(1)} %convolution_add_fusion.hidden, f32[14,1152]{1,0:T(8,128)S(1)} %pad_maximum_fusion.1.mods, bf16[144,1152]{1,0:T(8,128)(2,1)S(1)} %maximum_select_fusion.refs_0_, ...), custom_call_target="tpu_custom_call" | custom-call | flops 1783627776 | bytes 5308416 | tf_op jit(solution)/shard_map/pallas_call | solution.py:326
  102.5 7.0 %shard_map.150.refs_0_ = bf16[448,1152]{1,0:T(8,128)(2,1)S(1)} custom-call(s32[4]{0:T(128)S(1)} %pad_add_fusion.ids, bf16[24,448,72]{2,1,0:T(8,128)(2,1)S(1)} %copy-done.22, bf16[1152,576]{1,0:T(8,128)(2,1)S(1)} %get-tuple-element.63.proj), custom_call_target="tpu_custom_call" | custom-call | flops 1056964608 | bytes 5308416 | tf_op jit(solution)/shard_map/pallas_call | solution.py:326
  117.3 17.2 %collective-permute-done.20 = bf16[144,1152]{1,0:T(8,128)(2,1)S(1)} collective-permute-done((bf16[144,1152]{1,0:T(8,128)(2,1)S(1)}, bf16[144,1152]{1,0:T(8,128)(2,1)S(1)}, u32[]{:S(2)}, u32[]{:S(2)}) %collective-permute-start.20) | collective-permute-done | bytes 331808 | tf_op jit(solution)/shard_map/ppermute | solution.py:214
  145.7 11.1 %shard_map.151 = (f32[448,1152]{1,0:T(8,128)}, bf16[2,448,1152]{2,1,0:T(8,128)(2,1)}) custom-call(s32[4]{0:T(128)S(1)} %pad_add_fusion.ids, f32[448,1152]{1,0:T(8,128)} %copy-done.2, f32[14,1152]{1,0:T(8,128)S(1)} %pad_maximum_fusion.1.mods, bf16[448,1152]{1,0:T(8,128)(2,1)} %copy-done.12, bf16[448,1152]{1,0:T(8,128)(2,1)} %copy-done.33, ...), custom_call_target="tpu_custom_call" | custom-call | flops 2378170368 | bytes 5308416 | tf_op jit(solution)/shard_map/pallas_call | solution.py:326
  156.8 5.5 %collective-permute-done.25 = bf16[144,1152]{1,0:T(8,128)(2,1)S(1)} collective-permute-done((bf16[144,1152]{1,0:T(8,128)(2,1)S(1)}, bf16[144,1152]{1,0:T(8,128)(2,1)S(1)}, u32[]{:S(2)}, u32[]{:S(2)}) %collective-permute-start.25) | collective-permute-done | bytes 331808 | tf_op jit(solution)/shard_map/ppermute | solution.py:214
  170.4 9.1 %shard_map.152.refs_0_ = bf16[448,1152]{1,0:T(8,128)(2,1)} custom-call(s32[4]{0:T(128)S(1)} %pad_add_fusion.ids, bf16[2,448,1152]{2,1,0:T(8,128)(2,1)} %get-tuple-element.77.units, bf16[432,1152]{1,0:T(8,128)(2,1)S(1)} %constant_dynamic-update-slice_fusion.4.refs_6_.refs_0_.refs_2_, bf16[432,1152]{1,0:T(8,128)(2,1)S(1)} %collective-permute-done.14.refs_7_.refs_1_.refs_3_, ...), custom_call_target="tpu_custom_call" | custom-call | flops 2378170368 | bytes 5308416 | tf_op jit(solution)/shard_map/pallas_call | solution.py:326
  179.5 8.7 %collective-permute-done.31 = bf16[144,1152]{1,0:T(8,128)(2,1)S(1)} collective-permute-done((bf16[144,1152]{1,0:T(8,128)(2,1)S(1)}, bf16[144,1152]{1,0:T(8,128)(2,1)S(1)}, u32[]{:S(2)}, u32[]{:S(2)}) %collective-permute-start.31) | collective-permute-done | bytes 331808 | tf_op jit(solution)/shard_map/ppermute | solution.py:214
  189.2 4.5 %collective-permute-done.33.refs_12_.refs_4_ = bf16[576,1152]{1,0:T(8,128)(2,1)S(1)} collective-permute-done((bf16[576,1152]{1,0:T(8,128)(2,1)S(1)}, bf16[576,1152]{1,0:T(8,128)(2,1)S(1)}, u32[]{:S(2)}, u32[]{:S(2)}) %collective-permute-start.33) | collective-permute-done | bytes 1327136 | tf_op jit(solution)/shard_map/ppermute | solution.py:214
  200.3 22.5 %collective-permute-done.29.refs_1_ = bf16[448,1152]{1,0:T(8,128)(2,1)S(1)} collective-permute-done((bf16[448,1152]{1,0:T(8,128)(2,1)S(1)}, bf16[448,1152]{1,0:T(8,128)(2,1)S(1)}, u32[]{:S(2)}, u32[]{:S(2)}) %collective-permute-start.29) | collective-permute-done | bytes 1032224 | tf_op jit(solution)/shard_map/ppermute | solution.py:214
  223.8 10.8 %shard_map.153 = (f32[448,1152]{1,0:T(8,128)}, bf16[24,448,72]{2,1,0:T(8,128)(2,1)}, bf16[1152,576]{1,0:T(8,128)(2,1)}) custom-call(s32[4]{0:T(128)S(1)} %pad_add_fusion.ids, f32[448,1152]{1,0:T(8,128)} %get-tuple-element.76.hidden, f32[14,1152]{1,0:T(8,128)S(1)} %pad_maximum_fusion.1.mods, bf16[448,1152]{1,0:T(8,128)(2,1)S(1)} %copy-done.11, ...), custom_call_target="tpu_custom_call" | custom-call | flops 1783627776 | bytes 5308416 | tf_op jit(solution)/shard_map/pallas_call | solution.py:326
  237.8 8.0 %shard_map.154.refs_0_ = bf16[448,1152]{1,0:T(8,128)(2,1)} custom-call(s32[4]{0:T(128)S(1)} %pad_add_fusion.ids, bf16[24,448,72]{2,1,0:T(8,128)(2,1)S(1)} %copy-done.21, bf16[1152,576]{1,0:T(8,128)(2,1)S(1)} %copy-done.23), custom_call_target="tpu_custom_call" | custom-call | flops 1056964608 | bytes 5308416 | tf_op jit(solution)/shard_map/pallas_call | solution.py:326
  248.8 14.8 %collective-permute-done.41.refs_6_ = bf16[288,1152]{1,0:T(8,128)(2,1)S(1)} collective-permute-done((bf16[288,1152]{1,0:T(8,128)(2,1)}, bf16[288,1152]{1,0:T(8,128)(2,1)S(1)}, u32[]{:S(2)}, u32[]{:S(2)}) %collective-permute-start.41) | collective-permute-done | bytes 663584 | tf_op jit(solution)/shard_map/ppermute | solution.py:214
  264.4 8.0 %collective-permute-done.35.refs_1_ = bf16[448,1152]{1,0:T(8,128)(2,1)} collective-permute-done((bf16[448,1152]{1,0:T(8,128)(2,1)}, bf16[448,1152]{1,0:T(8,128)(2,1)}, u32[]{:S(2)}, u32[]{:S(2)}) %collective-permute-start.35) | collective-permute-done | bytes 1032224 | tf_op jit(solution)/shard_map/ppermute | solution.py:214
  275.0 11.4 %shard_map.155 = (f32[448,1152]{1,0:T(8,128)}, bf16[2,448,1152]{2,1,0:T(8,128)(2,1)}) custom-call(s32[4]{0:T(128)S(1)} %pad_add_fusion.ids, f32[448,1152]{1,0:T(8,128)} %get-tuple-element.89.hidden, f32[14,1152]{1,0:T(8,128)S(1)} %pad_maximum_fusion.1.mods, bf16[448,1152]{1,0:T(8,128)(2,1)} %shard_map.154.refs_0_, ...), custom_call_target="tpu_custom_call" | custom-call | flops 2378170368 | bytes 5308416 | tf_op jit(solution)/shard_map/pallas_call | solution.py:326
  287.5 8.0 %shard_map.156 = bf16[448,1152]{1,0:T(8,128)(2,1)S(1)} custom-call(s32[4]{0:T(128)S(1)} %pad_add_fusion.ids, bf16[2,448,1152]{2,1,0:T(8,128)(2,1)} %get-tuple-element.97.units, bf16[576,1152]{1,0:T(8,128)(2,1)} %get-tuple-element.120.refs_6_.refs_0_, bf16[576,1152]{1,0:T(8,128)(2,1)} %collective-permute-done.36.refs_7_.refs_1_, ...), custom_call_target="tpu_custom_call" | custom-call | flops 2378170368 | bytes 5308416 | tf_op jit(solution)/shard_map/pallas_call | solution.py:326
  297.3 10.4 %collective-permute-done.43 = bf16[224,1152]{1,0:T(8,128)(2,1)S(1)} collective-permute-done((bf16[224,1152]{1,0:T(8,128)(2,1)S(1)}, bf16[224,1152]{1,0:T(8,128)(2,1)S(1)}, u32[]{:S(2)}, u32[]{:S(2)}) %collective-permute-start.43) | collective-permute-done | bytes 516128 | tf_op jit(solution)/shard_map/ppermute | solution.py:214
  (229 shorter events, 106.1 us)
Async XLA Ops:
  6.9 80.0 %collective-permute-start.1 = (bf16[144,1152]{1,0:T(8,128)(2,1)S(1)}, bf16[144,1152]{1,0:T(8,128)(2,1)}, u32[]{:S(2)}, u32[]{:S(2)}) collective-permute-start(bf16[144,1152]{1,0:T(8,128)(2,1)S(1)} %maximum_select_fusion.refs_0_), channel_id=1, source_target_pairs={{0,16},{16,0},{1,17},{17,1},{2,18},{18,2},{3,19},{19,3},{4,20},{20... | collective-permute-start | bytes 995336 | tf_op jit(solution)/shard_map/ppermute | solution.py:214
  12.7 28.1 %all-to-all-start = ((bf16[8,1,144]{2,1,0:T(2,128)(2,1)}), bf16[8,1,144]{2,1,0:T(2,128)(2,1)S(1)}, u32[]{:S(2)}, u32[]{:S(2)}) async-start(bf16[8,1,144]{2,1,0:T(2,128)(2,1)} %copy.27), calls=%async_computation | async-start | bytes 16384 | tf_op jit(solution)/shard_map/all_to_all | solution.py:560
  49.3 30.7 %collective-permute-start.11 = (bf16[288,1152]{1,0:T(8,128)(2,1)S(1)}, bf16[288,1152]{1,0:T(8,128)(2,1)}, u32[]{:S(2)}, u32[]{:S(2)}) collective-permute-start(bf16[288,1152]{1,0:T(8,128)(2,1)S(1)} %collective-permute-done.6.refs_8_), channel_id=1, source_target_pairs={{0,1},{1,0},{2,3},{3,2},{4,5},{5,4},{6,7},{7,6},{8,9},{9,8},{10,11... | collective-permute-start | bytes 1990664 | tf_op jit(solution)/shard_map/ppermute | solution.py:214
  55.7 23.0 %collective-permute-start.10 = (bf16[144,1152]{1,0:T(8,128)(2,1)}, bf16[144,1152]{1,0:T(8,128)(2,1)}, u32[]{:S(2)}, u32[]{:S(2)}) collective-permute-start(bf16[144,1152]{1,0:T(8,128)(2,1)} %dynamic-slice_bitcast_fusion.3), channel_id=1, source_target_pairs={{0,4},{1,5},{2,6},{3,7},{4,0},{5,1},{6,2},{7,3},{8,12},{9,13},{10,... | collective-permute-start | bytes 995336 | tf_op jit(solution)/shard_map/ppermute | solution.py:214
  62.7 27.0 %collective-permute-start.5 = (bf16[288,1152]{1,0:T(8,128)(2,1)}, bf16[288,1152]{1,0:T(8,128)(2,1)}, u32[]{:S(2)}, u32[]{:S(2)}) collective-permute-start(bf16[288,1152]{1,0:T(8,128)(2,1)} %constant_dynamic-update-slice_fusion.refs_4_.refs_2_), channel_id=1, source_target_pairs={{0,16},{16,0},{1,17},{17,1},{2,18},{18,2},{3,19},{19,3},{4,20},{20... | collective-permute-start | bytes 1990664 | tf_op jit(solution)/shard_map/ppermute | solution.py:214
  86.9 26.6 %collective-permute-start.17 = (bf16[432,1152]{1,0:T(8,128)(2,1)S(1)}, bf16[432,1152]{1,0:T(8,128)(2,1)}, u32[]{:S(2)}, u32[]{:S(2)}) collective-permute-start(bf16[432,1152]{1,0:T(8,128)(2,1)S(1)} %constant_dynamic-update-slice_fusion.4.refs_6_.refs_0_.refs_2_), channel_id=1, source_target_pairs={{0,1},{1,0},{2,3},{3,2},{4,5},{5,4},{6,7},{7,6},{8,9},{9,8},{10,11... | collective-permute-start | bytes 2985992 | tf_op jit(solution)/shard_map/ppermute | solution.py:214
  89.8 23.6 %collective-permute-start.16 = (bf16[288,1152]{1,0:T(8,128)(2,1)}, bf16[288,1152]{1,0:T(8,128)(2,1)S(1)}, u32[]{:S(2)}, u32[]{:S(2)}) collective-permute-start(bf16[288,1152]{1,0:T(8,128)(2,1)} %copy-done.38), channel_id=1, source_target_pairs={{0,2},{1,3},{2,0},{3,1},{4,6},{5,7},{6,4},{7,5},{8,10},{9,11},{10,... | collective-permute-start | bytes 1990664 | tf_op jit(solution)/shard_map/ppermute | solution.py:214
  109.6 28.8 %collective-permute-start.13 = (bf16[448,1152]{1,0:T(8,128)(2,1)S(1)}, bf16[448,1152]{1,0:T(8,128)(2,1)S(1)}, u32[]{:S(2)}, u32[]{:S(2)}) collective-permute-start(bf16[448,1152]{1,0:T(8,128)(2,1)S(1)} %shard_map.150.refs_0_), channel_id=1, source_target_pairs={{0,8},{8,0},{1,9},{9,1},{2,10},{10,2},{3,11},{11,3},{4,12},{12,4},... | collective-permute-start | bytes 3096584 | tf_op jit(solution)/shard_map/ppermute | solution.py:214
  113.6 24.8 %collective-permute-start.22 = (bf16[432,1152]{1,0:T(8,128)(2,1)S(1)}, bf16[432,1152]{1,0:T(8,128)(2,1)S(1)}, u32[]{:S(2)}, u32[]{:S(2)}) collective-permute-start(bf16[432,1152]{1,0:T(8,128)(2,1)S(1)} %get-tuple-element.130.refs_10_.refs_4_), channel_id=1, source_target_pairs={{0,1},{1,0},{2,3},{3,2},{4,5},{5,4},{6,7},{7,6},{8,9},{9,8},{10,11... | collective-permute-start | bytes 2985992 | tf_op jit(solution)/shard_map/ppermute | solution.py:214
  115.7 24.9 %collective-permute-start.14 = (bf16[432,1152]{1,0:T(8,128)(2,1)S(1)}, bf16[432,1152]{1,0:T(8,128)(2,1)S(1)}, u32[]{:S(2)}, u32[]{:S(2)}) collective-permute-start(bf16[432,1152]{1,0:T(8,128)(2,1)S(1)} %constant_dynamic-update-slice_fusion.4.refs_6_.refs_0_.refs_2_), channel_id=1, source_target_pairs={{0,16},{16,0},{1,17},{17,1},{2,18},{18,2},{3,19},{19,3},{4,20},{20... | collective-permute-start | bytes 2985992 | tf_op jit(solution)/shard_map/ppermute | solution.py:214
  139.4 24.5 %collective-permute-start.27 = (bf16[432,1152]{1,0:T(8,128)(2,1)S(1)}, bf16[432,1152]{1,0:T(8,128)(2,1)S(1)}, u32[]{:S(2)}, u32[]{:S(2)}) collective-permute-start(bf16[432,1152]{1,0:T(8,128)(2,1)S(1)} %get-tuple-element.128.refs_8_.refs_6_), channel_id=1, source_target_pairs={{0,1},{1,0},{2,3},{3,2},{4,5},{5,4},{6,7},{7,6},{8,9},{9,8},{10,11... | collective-permute-start | bytes 2985992 | tf_op jit(solution)/shard_map/ppermute | solution.py:214
  140.6 23.3 %collective-permute-start.26 = (bf16[288,1152]{1,0:T(8,128)(2,1)S(1)}, bf16[288,1152]{1,0:T(8,128)(2,1)S(1)}, u32[]{:S(2)}, u32[]{:S(2)}) collective-permute-start(bf16[288,1152]{1,0:T(8,128)(2,1)S(1)} %get-tuple-element.127), channel_id=1, source_target_pairs={{0,2},{1,3},{2,0},{3,1},{4,6},{5,7},{6,4},{7,5},{8,10},{9,11},{10,... | collective-permute-start | bytes 1990664 | tf_op jit(solution)/shard_map/ppermute | solution.py:214
  164.1 29.6 %collective-permute-start.33 = (bf16[576,1152]{1,0:T(8,128)(2,1)S(1)}, bf16[576,1152]{1,0:T(8,128)(2,1)S(1)}, u32[]{:S(2)}, u32[]{:S(2)}) collective-permute-start(bf16[576,1152]{1,0:T(8,128)(2,1)S(1)} %get-tuple-element.124.refs_10_.refs_2_), channel_id=1, source_target_pairs={{0,1},{1,0},{2,3},{3,2},{4,5},{5,4},{6,7},{7,6},{8,9},{9,8},{10,11... | collective-permute-start | bytes 3981320 | tf_op jit(solution)/shard_map/ppermute | solution.py:214
  166.0 23.2 %collective-permute-start.32 = (bf16[288,1152]{1,0:T(8,128)(2,1)S(1)}, bf16[288,1152]{1,0:T(8,128)(2,1)S(1)}, u32[]{:S(2)}, u32[]{:S(2)}) collective-permute-start(bf16[288,1152]{1,0:T(8,128)(2,1)S(1)} %get-tuple-element.123), channel_id=1, source_target_pairs={{0,2},{1,3},{2,0},{3,1},{4,6},{5,7},{6,4},{7,5},{8,10},{9,11},{10,... | collective-permute-start | bytes 1990664 | tf_op jit(solution)/shard_map/ppermute | solution.py:214
  168.1 31.3 %collective-permute-start.30 = (bf16[576,1152]{1,0:T(8,128)(2,1)S(1)}, bf16[576,1152]{1,0:T(8,128)(2,1)S(1)}, u32[]{:S(2)}, u32[]{:S(2)}) collective-permute-start(bf16[576,1152]{1,0:T(8,128)(2,1)S(1)} %get-tuple-element.124.refs_10_.refs_2_), channel_id=1, source_target_pairs={{0,16},{16,0},{1,17},{17,1},{2,18},{18,2},{3,19},{19,3},{4,20},{20... | collective-permute-start | bytes 3981320 | tf_op jit(solution)/shard_map/ppermute | solution.py:214
  193.7 29.1 %collective-permute-start.34 = (bf16[576,1152]{1,0:T(8,128)(2,1)S(1)}, bf16[576,1152]{1,0:T(8,128)(2,1)S(1)}, u32[]{:S(2)}, u32[]{:S(2)}) collective-permute-start(bf16[576,1152]{1,0:T(8,128)(2,1)S(1)} %collective-permute-done.33.refs_12_.refs_4_), channel_id=1, source_target_pairs={{0,16},{16,0},{1,17},{17,1},{2,18},{18,2},{3,19},{19,3},{4,20},{20... | collective-permute-start | bytes 3981320 | tf_op jit(solution)/shard_map/ppermute | solution.py:214
  198.2 47.6 %collective-permute-start.38 = (bf16[576,1152]{1,0:T(8,128)(2,1)}, bf16[576,1152]{1,0:T(8,128)(2,1)}, u32[]{:S(2)}, u32[]{:S(2)}) collective-permute-start(bf16[576,1152]{1,0:T(8,128)(2,1)} %get-tuple-element.120.refs_6_.refs_0_), channel_id=1, source_target_pairs={{0,1},{1,0},{2,3},{3,2},{4,5},{5,4},{6,7},{7,6},{8,9},{9,8},{10,11... | collective-permute-start | bytes 3981320 | tf_op jit(solution)/shard_map/ppermute | solution.py:214
  198.5 24.2 %collective-permute-start.29 = (bf16[448,1152]{1,0:T(8,128)(2,1)S(1)}, bf16[448,1152]{1,0:T(8,128)(2,1)S(1)}, u32[]{:S(2)}, u32[]{:S(2)}) collective-permute-start(bf16[448,1152]{1,0:T(8,128)(2,1)S(1)} %copy-done.11), channel_id=1, source_target_pairs={{0,8},{8,0},{1,9},{9,1},{2,10},{10,2},{3,11},{11,3},{4,12},{12,4},... | collective-permute-start | bytes 3096584 | tf_op jit(solution)/shard_map/ppermute | solution.py:214
  198.8 47.1 %collective-permute-start.37 = (bf16[288,1152]{1,0:T(8,128)(2,1)S(1)}, bf16[288,1152]{1,0:T(8,128)(2,1)}, u32[]{:S(2)}, u32[]{:S(2)}) collective-permute-start(bf16[288,1152]{1,0:T(8,128)(2,1)S(1)} %get-tuple-element.119), channel_id=1, source_target_pairs={{0,2},{1,3},{2,0},{3,1},{4,6},{5,7},{6,4},{7,5},{8,10},{9,11},{10,... | collective-permute-start | bytes 1990664 | tf_op jit(solution)/shard_map/ppermute | solution.py:214
  199.4 64.9 %collective-permute-start.36 = (bf16[576,1152]{1,0:T(8,128)(2,1)}, bf16[576,1152]{1,0:T(8,128)(2,1)}, u32[]{:S(2)}, u32[]{:S(2)}) collective-permute-start(bf16[576,1152]{1,0:T(8,128)(2,1)} %get-tuple-element.120.refs_6_.refs_0_), channel_id=1, source_target_pairs={{0,16},{16,0},{1,17},{17,1},{2,18},{18,2},{3,19},{19,3},{4,20},{20... | collective-permute-start | bytes 3981320 | tf_op jit(solution)/shard_map/ppermute | solution.py:214
  245.8 26.5 %collective-permute-start.39 = (bf16[576,1152]{1,0:T(8,128)(2,1)}, bf16[576,1152]{1,0:T(8,128)(2,1)}, u32[]{:S(2)}, u32[]{:S(2)}) collective-permute-start(bf16[576,1152]{1,0:T(8,128)(2,1)} %collective-permute-done.38.refs_8_.refs_2_), channel_id=1, source_target_pairs={{0,16},{16,0},{1,17},{17,1},{2,18},{18,2},{3,19},{19,3},{4,20},{20... | collective-permute-start | bytes 3981320 | tf_op jit(solution)/shard_map/ppermute | solution.py:214
  248.0 24.4 %collective-permute-start.35 = (bf16[448,1152]{1,0:T(8,128)(2,1)}, bf16[448,1152]{1,0:T(8,128)(2,1)}, u32[]{:S(2)}, u32[]{:S(2)}) collective-permute-start(bf16[448,1152]{1,0:T(8,128)(2,1)} %shard_map.154.refs_0_), channel_id=1, source_target_pairs={{0,8},{8,0},{1,9},{9,1},{2,10},{10,2},{3,11},{11,3},{4,12},{12,4},... | collective-permute-start | bytes 3096584 | tf_op jit(solution)/shard_map/ppermute | solution.py:214
  248.2 38.2 %collective-permute-start.40 = (bf16[288,1152]{1,0:T(8,128)(2,1)}, bf16[288,1152]{1,0:T(8,128)(2,1)}, u32[]{:S(2)}, u32[]{:S(2)}) collective-permute-start(bf16[288,1152]{1,0:T(8,128)(2,1)} %collective-permute-done.37.refs_4_), channel_id=1, source_target_pairs={{0,16},{16,0},{1,17},{17,1},{2,18},{18,2},{3,19},{19,3},{4,20},{20... | collective-permute-start | bytes 1990664 | tf_op jit(solution)/shard_map/ppermute | solution.py:214
  263.6 22.8 %collective-permute-start.42 = (bf16[288,1152]{1,0:T(8,128)(2,1)S(1)}, bf16[288,1152]{1,0:T(8,128)(2,1)}, u32[]{:S(2)}, u32[]{:S(2)}) collective-permute-start(bf16[288,1152]{1,0:T(8,128)(2,1)S(1)} %collective-permute-done.41.refs_6_), channel_id=1, source_target_pairs={{0,16},{16,0},{1,17},{17,1},{2,18},{18,2},{3,19},{19,3},{4,20},{20... | collective-permute-start | bytes 1990664 | tf_op jit(solution)/shard_map/ppermute | solution.py:214
  (68 other events, 776.8 us)
where the time goes:
time: 319 us; the launch traced here: 318 us
  waiting for transfers between devices  118 us (37%)
  Pallas kernels  73.9 us (23%)
  starting transfers between devices  56.9 us (18%)
  local copies, waits for them, and re-layouts  43.8 us (14%)
  other arithmetic  14.9 us (5%)
  between operations  5.85 us (2%)
  matrix products  4.3 us (1%)
    ppermute x44, waiting for transfers between devices, exchange(): return lax.ppermute(block, axis, [(at, at ^ bit) for at in range(count)])  118 us
    pallas_call x8, Pallas kernels, kernel_call(): pl.pallas_call(body, out_shape=outs, in_specs=specs, out_specs=jax.tree.m...  73.9 us
    ppermute x44, starting transfers between devices, exchange(): return lax.ppermute(block, axis, [(at, at ^ bit) for at in range(count)])  47.2 us
    unnamed x101, local copies, waits for them, and re-layouts  18.4 us
  transfers between devices with their start and end apart: 47, of which 17 were waited for; matrix products, arithmetic and copies ran while one was open for 12% of the time, Pallas kernels for 21%

commit v1 on v0

--- a/solution.py
+++ b/solution.py
@@ -35,6 +35,15 @@
 
 def modulate(values, shift, scale):
     return layer_norm(values) * (1.0 + scale[:, None, :]) + shift[:, None, :]
+
+
+def position_values(row_count, width):
+    half_width = width // 2
+    frequency = np.exp(
+        np.arange(half_width, dtype=np.float32) * np.float32(-math.log(10000.0) / half_width)
+    )
+    angles = np.arange(row_count, dtype=np.float32)[:, None] * frequency[None, :]
+    return np.concatenate([np.sin(angles), np.cos(angles)], axis=1).astype(np.float32)
 
 
 def position_table(row_count, width):
@@ -214,10 +223,6 @@
     return lax.ppermute(block, axis, [(at, at ^ bit) for at in range(count)])
 
 
-def after(value, *earlier):
-    return lax.optimization_barrier((value, *earlier))[0]
-
-
 HOLDS = {"own": (0,), "two": (4,), "pair": (0, 4), "four": (2, 6)}
 
 PLAN = (
@@ -227,8 +232,8 @@
     ((("pair", 1), ("own", 2)), (("two", 1), ("own", 2), ("own", 3))),
     ((("pair", 2), ("own", 3)), (("four", 1), ("two", 2))),
     ((("pair", 3), ("own", 4)), (("four", 2), ("two", 3))),
-    ((("pair", 4), ("own", 5)), (("four", 3), ("pair", 4))),
-    ((("pair", 5),), (("four", 4), ("pair", 5))),
+    ((("pair", 4), ("own", 5)), (("four", 3), ("pair", 4), ("own", 5))),
+    ((("pair", 5),), (("four", 4), ("two", 5))),
     ((), (("four", 5),)),
 )
 READY = ((0,), (1, 2), (3,), (), (4, 5))
@@ -236,13 +241,12 @@
 
 class Stream:
     def __init__(self, make_own):
-        self.make_own, self.at, self.last = make_own, 0, None
+        self.make_own, self.at = make_own, 0
         self.values, self.arrived, self.sent = {}, {}, ()
         self.blocks = [[] for _ in make_own]
 
-    def hand_over(self, array, parts, flip, anchor):
-        earlier = []
-        other = self.last = exchange(after(array, *earlier) if earlier else array, "guide", 1)
+    def hand_over(self, array, parts, flip):
+        other = exchange(array, "guide", 1)
         at = 0
         for kind, piece in parts:
             for distance in HOLDS[kind]:
@@ -263,20 +267,18 @@
                 values["pair", piece] = jnp.concatenate([values["own", piece], value], axis=0)
             elif kind == "pair":
                 values["four", piece] = value
-        came = arrived.get("x")
-        self.arrived, anchor = {}, None
+        self.arrived = {}
         source = [values[part] for part in over_x]
         if source:
             source = source[0] if len(source) == 1 else jnp.concatenate(source, axis=0)
             self.arrived["x", ""] = exchange(source, "batch", 1)
         for kind, piece in over_z:
-            sent = exchange(values[kind, piece], "batch", 4 if kind == "own" else 2)
-            self.arrived[kind, piece] = sent
-            anchor = sent if anchor is None else anchor
+            bit = 4 if kind == "own" else 2
+            self.arrived[kind, piece] = exchange(values[kind, piece], "batch", bit)
         if ("x", "") in arrived:
-            self.hand_over(arrived["x", ""], self.sent, 1, None)
+            self.hand_over(arrived["x", ""], self.sent, 1)
         if over_x:
-            self.hand_over(source, over_x, 0, anchor)
+            self.hand_over(source, over_x, 0)
         self.sent = over_x
 
     def operands(self, piece):
@@ -317,12 +319,11 @@
     )
 
 
-def kernel_call(body, outs, scratch, operands, buffers, flops, bytes_moved):
+def kernel_call(body, outs, scratch, operands, buffers, fetches, flops, bytes_moved):
     specs = [pl.BlockSpec(memory_space=pltpu.SMEM)]
     specs += [pl.BlockSpec(memory_space=pltpu.VMEM) for _ in operands[1:]]
     specs += [pl.BlockSpec(memory_space=pl.ANY) for _ in buffers]
-    if buffers:
-        scratch = scratch + [pltpu.SemaphoreType.DMA((16,))]
+    scratch = scratch + [pltpu.SemaphoreType.DMA((16,))] * fetches
     return pl.pallas_call(
         body,
         out_shape=outs,
@@ -347,20 +348,19 @@
     )
 
 
-def qkv_kernel(places, array_count, layer, heads, branch_count, ids, hidden, mods, *refs):
+def attention_kernel(places, array_count, layer, heads, branch_count, ids, hidden, mods, *refs):
     branches, refs = refs[:branch_count], refs[branch_count:]
     buffers, refs = refs[:array_count], refs[array_count:]
     hidden_out = None
     if branches:
         hidden_out, refs = refs[0], refs[1:]
-    heads_out, proj_out, weights, normed, projected, arrivals = refs
-    width = hidden.shape[1]
+    partial, weights, normed, projected, split, attended, arrivals = refs
+    width, keys = hidden.shape[1], hidden.shape[0]
     half = width // 2
     copies = fetch(weights, [ids[1], 1 - ids[1]], buffers, places, ids[0], arrivals)
     enter(hidden, branches, mods, 6 * layer, hidden_out, normed)
     for copy in copies:
         copy.wait()
-    proj_out[...] = weights[1, :, half:]
 
     def step(at, carry):
         lo = pl.multiple_of(at * 384, 128)
@@ -374,34 +374,23 @@
         normed[...], weights[1, :, :half], preferred_element_type=jnp.float32
     ).astype(jnp.bfloat16)
     for at in range(3 * heads):
-        heads_out[at] = projected[:, at * HDIM : (at + 1) * HDIM]
-
-
-def attention_kernel(heads, ids, heads_in, proj, partial, attended):
-    keys = heads_in.shape[1]
+        split[at] = projected[:, at * HDIM : (at + 1) * HDIM]
     factor = math.log2(math.e) / math.sqrt(HDIM)
     live = lax.broadcasted_iota(jnp.int32, (1, keys), 1) < ids[3]
     for at in range(heads):
-        scores = dot_nt(heads_in[at], heads_in[heads + at])
+        scores = dot_nt(split[at], split[heads + at])
         scores = jnp.where(live, scores * factor, -jnp.inf)
         raised = jnp.exp2(scores - jnp.max(scores, axis=-1, keepdims=True))
         total = jnp.sum(raised, axis=-1, keepdims=True)
         out = jnp.dot(
-            raised.astype(jnp.bfloat16), heads_in[2 * heads + at], preferred_element_type=jnp.float32
+            raised.astype(jnp.bfloat16), split[2 * heads + at], preferred_element_type=jnp.float32
         )
         attended[:, at * HDIM : (at + 1) * HDIM] = (out / total).astype(jnp.bfloat16)
-    partial[...] = dot_nt(attended[...], proj[...]).astype(jnp.bfloat16)
-
-
-def up_kernel(places, array_count, layer, ids, hidden, mods, *refs):
-    branches, refs = refs[:2], refs[2:]
-    buffers, refs = refs[:array_count], refs[array_count:]
-    hidden_out, units, weights, normed, arrivals = refs
-    width = hidden.shape[1]
-    copies = fetch(weights, [0, 1], buffers, places, ids[0], arrivals)
-    enter(hidden, branches, mods, 6 * layer + 3, hidden_out, normed)
-    for copy in copies:
-        copy.wait()
+    partial[...] = dot_nt(attended[...], weights[1, :, half:]).astype(jnp.bfloat16)
+
+
+def expand(normed, weights, units):
+    width = normed.shape[1]
     for half in range(2):
 
         def step(at, carry):
@@ -418,11 +407,8 @@
         lax.fori_loop(0, width // 384, step, 0)
 
 
-def down_kernel(places, array_count, ids, units, *refs):
-    buffers, (partial, weights, arrivals) = refs[:array_count], refs[array_count:]
+def contract(units, weights, partial):
     width = partial.shape[1]
-    for copy in fetch(weights, [0, 1], buffers, places, ids[0], arrivals):
-        copy.wait()
 
     def step(at, carry):
         lo = pl.multiple_of(at * 384, 128)
@@ -432,6 +418,39 @@
         return carry
 
     lax.fori_loop(0, width // 384, step, 0)
+
+
+def up_kernel(places, array_count, layer, ids, hidden, mods, *refs):
+    branches, refs = refs[:2], refs[2:]
+    buffers, refs = refs[:array_count], refs[array_count:]
+    hidden_out, units, weights, normed, arrivals = refs
+    copies = fetch(weights, [0, 1], buffers, places, ids[0], arrivals)
+    enter(hidden, branches, mods, 6 * layer + 3, hidden_out, normed)
+    for copy in copies:
+        copy.wait()
+    expand(normed, weights, units)
+
+
+def down_kernel(places, array_count, ids, units, *refs):
+    buffers, (partial, weights, arrivals) = refs[:array_count], refs[array_count:]
+    for copy in fetch(weights, [0, 1], buffers, places, ids[0], arrivals):
+        copy.wait()
+    contract(units, weights, partial)
+
+
+def mlp_kernel(places, counts, layer, ids, hidden, mods, *refs):
+    branches, refs = refs[:2], refs[2:]
+    ups, downs, refs = refs[: counts[0]], refs[counts[0] : sum(counts)], refs[sum(counts) :]
+    hidden_out, partial, up_weights, down_weights, units, normed, arrivals, more_arrivals = refs
+    up_copies = fetch(up_weights, [0, 1], ups, places[0], ids[0], arrivals)
+    down_copies = fetch(down_weights, [0, 1], downs, places[1], ids[0], more_arrivals)
+    enter(hidden, branches, mods, 6 * layer + 3, hidden_out, normed)
+    for copy in up_copies:
+        copy.wait()
+    expand(normed, up_weights, units)
+    for copy in down_copies:
+        copy.wait()
+    contract(units, down_weights, partial)
 
 
 def modulation_sums(columns, modulation_weight, final_modulation):
@@ -504,29 +523,27 @@
     normed = pltpu.VMEM((max_len, width), bf16)
 
     def attention_block(layer, hidden, mods, branches):
-        outs = [shape((3 * heads, max_len, HDIM), bf16), shape((width, half), bf16)]
+        outs = [shape((max_len, width), bf16)]
         if branches:
             outs = [shape((max_len, width), f32)] + outs
         arrays, places = stream.operands(3 * layer)
         results = kernel_call(
-            functools.partial(qkv_kernel, places, len(arrays), layer, heads, len(branches)),
+            functools.partial(attention_kernel, places, len(arrays), layer, heads, len(branches)),
             outs,
-            [two_weights, normed, pltpu.VMEM((max_len, 3 * half), bf16)],
+            [
+                two_weights,
+                normed,
+                pltpu.VMEM((max_len, 3 * half), bf16),
+                pltpu.VMEM((3 * heads, max_len, HDIM), bf16),
+                pltpu.VMEM((max_len, half), bf16),
+            ],
             [ids, hidden, mods, *branches],
             arrays,
-            2 * max_len * width * 3 * half,
+            1,
+            2 * max_len * width * 4 * half + 4 * max_len * max_len * half,
             weight_bytes,
         )
-        partial = kernel_call(
-            functools.partial(attention_kernel, heads),
-            shape((max_len, width), bf16),
-            [pltpu.VMEM((max_len, half), bf16)],
-            [ids, *results[-2:]],
-            [],
-            4 * max_len * max_len * half + 2 * max_len * half * width,
-            weight_bytes,
-        )
-        return results[0] if branches else hidden, partial
+        return results[0] if branches else hidden, results[-1]
 
     def both(partial):
         return [partial, exchange(partial, "tensor", 1)]
@@ -539,6 +556,7 @@
             [two_weights, normed],
             [ids, hidden, mods, *branches],
             arrays,
+            1,
             4 * max_len * width * width,
             weight_bytes,
         )
@@ -551,8 +569,25 @@
             [two_weights],
             [ids, units],
             arrays,
+            1,
             4 * max_len * width * width,
             weight_bytes,
+        )
+
+    def mlp_block(layer, hidden, mods, branches):
+        arrays, places = stream.operands(3 * layer + 1)
+        more_arrays, more_places = stream.operands(3 * layer + 2)
+        return kernel_call(
+            functools.partial(
+                mlp_kernel, (places, more_places), (len(arrays), len(more_arrays)), layer
+            ),
+            [shape((max_len, width), f32), shape((max_len, width), bf16)],
+            [two_weights, two_weights, pltpu.VMEM((2, max_len, width), bf16), normed],
+            [ids, hidden, mods, *branches],
+            arrays + more_arrays,
+            2,
+            8 * max_len * width * width,
+            2 * weight_bytes,
         )
 
     activated = jax.nn.silu(condition[0]).astype(bf16).reshape(-1, width_piece)
@@ -561,26 +596,25 @@
     stream.step(columns)
     sums = modulation_sums(columns, modulation_weight, final_modulation)
     mine = jnp.sum(lax.all_to_all(sums, "batch", 0, 0, tiled=True), axis=0)
-    stream.step()
     hidden = jnp.einsum(
         "pl,pd->ld", latents[0], embed_weight, precision=lax.Precision.HIGHEST
-    ) + position_table(max_len, width)
+    ) + jnp.asarray(position_values(max_len, width))
     stream.step(mine, hidden)
     mods = all_columns(mine)
+    stream.step(mods)
     hidden, partial = attention_block(0, hidden, mods, [])
     stream.step(partial)
     branches = both(partial)
     stream.step(branches)
     hidden, units = up_block(0, hidden, mods, branches)
     stream.step(units)
-    partial = down_block(0, units)
-    stream.step(partial)
-    hidden, partial = attention_block(1, hidden, mods, both(partial))
+    branches = both(down_block(0, units))
+    stream.step(branches)
+    hidden, partial = attention_block(1, hidden, mods, branches)
     stream.step(partial)
     branches = both(partial)
     stream.step()
-    hidden, units = up_block(1, hidden, mods, branches)
-    partial = down_block(1, units)
+    hidden, partial = mlp_block(1, hidden, mods, branches)
     own_start = tensor_at * rows_own
     mine = lax.dynamic_slice_in_dim(partial, own_start, rows_own, 0)
     theirs = exchange(

time: 319 us -> 295 us (0.925)
  waiting for transfers between devices: 118 us -> 97.8 us
  Pallas kernels: 73.9 us -> 84.2 us
  other arithmetic: 14.9 us -> 4.79 us
  local copies, waits for them, and re-layouts: 43.8 us -> 40 us
    ppermute x44, waiting for transfers between devices: 118 us -> 84.2 us  [exchange(): return lax.ppermute(block, axis, [(at, at ^ bit) for at in range(count)])]
    all_to_all x1, waiting for transfers between devices: 0.54 us -> 13.6 us  [fast_local(): mine = jnp.sum(lax.all_to_all(sums, 'batch', 0, 0, tiled=True), axis=0)]
    pallas_call x8 -> x5, Pallas kernels: 73.9 us -> 84.2 us  [kernel_call(): pl.pallas_call(body, out_shape=outs, in_specs=specs, out_specs=jax.tree.m...]
    sin x1 -> x0, other arithmetic: 5.79 us -> none  [position_table(): return jnp.concatenate([jnp.sin(angles), jnp.cos(angles)], axis=1)]
    unnamed x101 -> x95, local copies, waits for them, and re-layouts: 18.4 us -> 18.9 us
  transfers between devices with their start and end apart: 47 -> 47, of which waited for: 17 -> 12; matrix products, arithmetic and copies ran while one was open for 12% -> 7% of each run, Pallas kernels for 21% -> 24%
where the time goes in v1:
time: 295 us; the launch traced here: 293 us
  waiting for transfers between devices  97.8 us (33%)
  Pallas kernels  84.2 us (29%)
  starting transfers between devices  55 us (19%)
  local copies, waits for them, and re-layouts  40 us (14%)
  between operations  5.95 us (2%)
  matrix products  5.64 us (2%)
  other arithmetic  4.79 us (2%)
    pallas_call x5, Pallas kernels, kernel_call(): pl.pallas_call(body, out_shape=outs, in_specs=specs, out_specs=jax.tree.m...  84.2 us
    ppermute x44, waiting for transfers between devices, exchange(): return lax.ppermute(block, axis, [(at, at ^ bit) for at in range(count)])  84.2 us
    ppermute x44, starting transfers between devices, exchange(): return lax.ppermute(block, axis, [(at, at ^ bit) for at in range(count)])  45.5 us
    unnamed x95, local copies, waits for them, and re-layouts  18.9 us
    all_to_all x1, waiting for transfers between devices, fast_local(): mine = jnp.sum(lax.all_to_all(sums, 'batch', 0, 0, tiled=True), axis=0)  13.6 us
  transfers between devices with their start and end apart: 47, of which 12 were waited for; matrix products, arithmetic and copies ran while one was open for 7% of the time, Pallas kernels for 24%

profile of v1, /device:TPU:1, one launch (start us, length us, event | category | flops | bytes accessed | tf_op | source)
XLA Modules:
  0.0 293.5 jit_solution(6260681249944899043)
XLA Ops:
  0.6 2.0 fusion.22
  6.8 3.2 %collective-permute-start.2 = (bf16[144,1152]{1,0:T(8,128)(2,1)S(1)}, bf16[144,1152]{1,0:T(8,128)(2,1)}, u32[]{:S(2)}, u32[]{:S(2)}) collective-permute-start(bf16[144,1152]{1,0:T(8,128)(2,1)S(1)} %maximum_select_fusion.refs_0_), channel_id=1, source_target_pairs={{0,4},{1,5},{2,6},{3,7},{4,0},{5,1},{6,2},{7,3},{8,12},{9,13},{10,... | collective-permute-start | bytes 995336 | tf_op jit(solution)/shard_map/ppermute | solution.py:223
  12.0 3.3 %all-to-all-start = ((bf16[8,1,144]{2,1,0:T(2,128)(2,1)}), bf16[8,1,144]{2,1,0:T(2,128)(2,1)S(1)}, u32[]{:S(2)}, u32[]{:S(2)}) async-start(bf16[8,1,144]{2,1,0:T(2,128)(2,1)} %copy.28), calls=%async_computation | async-start | bytes 16384 | tf_op jit(solution)/shard_map/all_to_all | solution.py:595
  15.3 2.2 fusion.21
  17.6 2.5 fusion.20
  20.8 4.8 %convolution_add_fusion.hidden = f32[448,1152]{1,0:T(8,128)} fusion(f32[448,1152]{1,0:T(8,128)} %constant.70.clone, f32[16,1152]{1,0:T(8,128)S(1)} %copy-done.37, f32[1,16,448]{2,1,0:T(8,128)S(1)} %copy-done.38), kind=kOutput, calls=%fused_computation | convolution fusion | flops 99606528 | bytes 4231168 | tf_op jit(solution)/shard_map/pl,pd->ld/dot_general | solution.py:599
  34.6 3.7 %all-to-all-start.1 = ((f32[8,14,576]{2,1,0:T(8,128)}), f32[8,14,576]{2,1,0:T(8,128)S(1)}, u32[]{:S(2)}, u32[]{:S(2)}) async-start(f32[8,14,576]{2,1,0:T(8,128)} %copy.30), calls=%async_computation.1 | async-start | bytes 655360 | tf_op jit(solution)/shard_map/all_to_all | solution.py:598
  38.5 13.6 %all-to-all-done.1 = f32[8,14,576]{2,1,0:T(8,128)S(1)} async-done(((f32[8,14,576]{2,1,0:T(8,128)}), f32[8,14,576]{2,1,0:T(8,128)S(1)}, u32[]{:S(2)}, u32[]{:S(2)}) %all-to-all-start.1) | async-done | bytes 258080 | tf_op jit(solution)/shard_map/all_to_all | solution.py:598
  53.5 3.4 %collective-permute-start.1 = (bf16[144,1152]{1,0:T(8,128)(2,1)S(1)}, bf16[144,1152]{1,0:T(8,128)(2,1)}, u32[]{:S(2)}, u32[]{:S(2)}) collective-permute-start(bf16[144,1152]{1,0:T(8,128)(2,1)S(1)} %maximum_select_fusion.refs_0_), channel_id=1, source_target_pairs={{0,16},{16,0},{1,17},{17,1},{2,18},{18,2},{3,19},{19,3},{4,20},{20... | collective-permute-start | bytes 995336 | tf_op jit(solution)/shard_map/ppermute | solution.py:223
  59.0 15.3 %collective-permute-done.10 = bf16[144,1152]{1,0:T(8,128)(2,1)S(1)} collective-permute-done((bf16[144,1152]{1,0:T(8,128)(2,1)}, bf16[144,1152]{1,0:T(8,128)(2,1)S(1)}, u32[]{:S(2)}, u32[]{:S(2)}) %collective-permute-start.10) | collective-permute-done | bytes 331808 | tf_op jit(solution)/shard_map/ppermute | solution.py:223
  90.0 16.6 %shard_map.158.refs_0_ = bf16[448,1152]{1,0:T(8,128)(2,1)S(1)} custom-call(s32[4]{0:T(128)S(1)} %pad_add_fusion.ids, f32[448,1152]{1,0:T(8,128)S(1)} %copy-done.2, f32[14,1152]{1,0:T(8,128)S(1)} %pad_maximum_fusion.1.mods, bf16[144,1152]{1,0:T(8,128)(2,1)S(1)} %maximum_select_fusion.refs_0_, bf16[144,1152]{1,0:T(8,128)(2,1)} %collective-permute-done.1.refs_1_, ...), custom_call_target="tpu_custom_call" | custom-call | flops 2840592384 | bytes 5308416 | tf_op jit(solution)/shard_map/pallas_call | solution.py:327
  112.6 16.6 %collective-permute-done.20 = bf16[144,1152]{1,0:T(8,128)(2,1)S(1)} collective-permute-done((bf16[144,1152]{1,0:T(8,128)(2,1)S(1)}, bf16[144,1152]{1,0:T(8,128)(2,1)S(1)}, u32[]{:S(2)}, u32[]{:S(2)}) %collective-permute-start.20) | collective-permute-done | bytes 331808 | tf_op jit(solution)/shard_map/ppermute | solution.py:223
  129.2 1.9 collective-permute-start.19
  135.7 2.1 collective-permute-start.25
  139.5 24.7 %shard_map.159 = (f32[448,1152]{1,0:T(8,128)}, bf16[2,448,1152]{2,1,0:T(8,128)(2,1)}) custom-call(s32[4]{0:T(128)S(1)} %pad_add_fusion.ids, f32[448,1152]{1,0:T(8,128)} %convolution_add_fusion.hidden, f32[14,1152]{1,0:T(8,128)S(1)} %pad_maximum_fusion.1.mods, bf16[448,1152]{1,0:T(8,128)(2,1)} %copy-done.14, bf16[448,1152]{1,0:T(8,128)(2,1)} %copy-done.32, ...), custom_call_target="tpu_custom_call" | custom-call | flops 2378170368 | bytes 5308416 | tf_op jit(solution)/shard_map/pallas_call | solution.py:327
  167.9 9.2 %shard_map.160.refs_0_ = bf16[448,1152]{1,0:T(8,128)(2,1)} custom-call(s32[4]{0:T(128)S(1)} %pad_add_fusion.ids, bf16[2,448,1152]{2,1,0:T(8,128)(2,1)} %get-tuple-element.72.units, bf16[432,1152]{1,0:T(8,128)(2,1)S(1)} %constant_dynamic-update-slice_fusion.4.refs_6_.refs_0_.refs_2_, bf16[432,1152]{1,0:T(8,128)(2,1)S(1)} %collective-permute-done.14.refs_7_.refs_1_.refs_3_, ...), custom_call_target="tpu_custom_call" | custom-call | flops 2378170368 | bytes 5308416 | tf_op jit(solution)/shard_map/pallas_call | solution.py:327
  181.2 18.1 %collective-permute-done.31 = bf16[144,1152]{1,0:T(8,128)(2,1)S(1)} collective-permute-done((bf16[144,1152]{1,0:T(8,128)(2,1)S(1)}, bf16[144,1152]{1,0:T(8,128)(2,1)S(1)}, u32[]{:S(2)}, u32[]{:S(2)}) %collective-permute-start.31) | collective-permute-done | bytes 331808 | tf_op jit(solution)/shard_map/ppermute | solution.py:223
  199.3 2.2 collective-permute-done.32
  209.6 19.1 %shard_map.161 = (f32[448,1152]{1,0:T(8,128)}, bf16[448,1152]{1,0:T(8,128)(2,1)}) custom-call(s32[4]{0:T(128)S(1)} %pad_add_fusion.ids, f32[448,1152]{1,0:T(8,128)} %get-tuple-element.71.hidden, f32[14,1152]{1,0:T(8,128)S(1)} %pad_maximum_fusion.1.mods, bf16[448,1152]{1,0:T(8,128)(2,1)S(1)} %copy-done.3, bf16[448,1152]{1,0:T(8,128)(2,1)} %copy-done.33, ...), custom_call_target="tpu_custom_call" | custom-call | flops 2840592384 | bytes 5308416 | tf_op jit(solution)/shard_map/pallas_call | solution.py:327
  232.4 12.9 %collective-permute-done.41.refs_20_ = bf16[288,1152]{1,0:T(8,128)(2,1)} collective-permute-done((bf16[288,1152]{1,0:T(8,128)(2,1)}, bf16[288,1152]{1,0:T(8,128)(2,1)}, u32[]{:S(2)}, u32[]{:S(2)}) %collective-permute-start.41) | collective-permute-done | bytes 663584 | tf_op jit(solution)/shard_map/ppermute | solution.py:223
  248.4 5.4 %collective-permute-done.35.refs_1_ = bf16[448,1152]{1,0:T(8,128)(2,1)} collective-permute-done((bf16[448,1152]{1,0:T(8,128)(2,1)}, bf16[448,1152]{1,0:T(8,128)(2,1)}, u32[]{:S(2)}, u32[]{:S(2)}) %collective-permute-start.35) | collective-permute-done | bytes 1032224 | tf_op jit(solution)/shard_map/ppermute | solution.py:223
  256.2 14.5 %shard_map.162 = (f32[448,1152]{1,0:T(8,128)}, bf16[448,1152]{1,0:T(8,128)(2,1)}) custom-call(s32[4]{0:T(128)S(1)} %pad_add_fusion.ids, f32[448,1152]{1,0:T(8,128)} %get-tuple-element.84.hidden, f32[14,1152]{1,0:T(8,128)S(1)} %pad_maximum_fusion.1.mods, bf16[448,1152]{1,0:T(8,128)(2,1)} %get-tuple-element.85.refs_0_, ...), custom_call_target="tpu_custom_call" | custom-call | flops 4756340736 | bytes 10616832 | tf_op jit(solution)/shard_map/pallas_call | solution.py:327
  274.5 9.1 %collective-permute-done.43 = bf16[224,1152]{1,0:T(8,128)(2,1)S(1)} collective-permute-done((bf16[224,1152]{1,0:T(8,128)(2,1)S(1)}, bf16[224,1152]{1,0:T(8,128)(2,1)S(1)}, u32[]{:S(2)}, u32[]{:S(2)}) %collective-permute-start.43) | collective-permute-done | bytes 516128 | tf_op jit(solution)/shard_map/ppermute | solution.py:223
  286.1 2.5 collective-permute-start.44
  (218 shorter events, 78.3 us)
Async XLA Ops:
  29.9 22.1 %collective-permute-start.6 = (bf16[288,1152]{1,0:T(8,128)(2,1)}, bf16[288,1152]{1,0:T(8,128)(2,1)}, u32[]{:S(2)}, u32[]{:S(2)}) collective-permute-start(bf16[288,1152]{1,0:T(8,128)(2,1)} %get-tuple-element.125), channel_id=1, source_target_pairs={{0,2},{1,3},{2,0},{3,1},{4,6},{5,7},{6,4},{7,5},{8,10},{9,11},{10,... | collective-permute-start | bytes 1990664 | tf_op jit(solution)/shard_map/ppermute | solution.py:223
  52.1 23.8 %collective-permute-start.11 = (bf16[288,1152]{1,0:T(8,128)(2,1)}, bf16[288,1152]{1,0:T(8,128)(2,1)}, u32[]{:S(2)}, u32[]{:S(2)}) collective-permute-start(bf16[288,1152]{1,0:T(8,128)(2,1)} %collective-permute-done.6.refs_8_), channel_id=1, source_target_pairs={{0,1},{1,0},{2,3},{3,2},{4,5},{5,4},{6,7},{7,6},{8,9},{9,8},{10,11... | collective-permute-start | bytes 1990664 | tf_op jit(solution)/shard_map/ppermute | solution.py:223
  53.5 26.3 %collective-permute-start.1 = (bf16[144,1152]{1,0:T(8,128)(2,1)S(1)}, bf16[144,1152]{1,0:T(8,128)(2,1)}, u32[]{:S(2)}, u32[]{:S(2)}) collective-permute-start(bf16[144,1152]{1,0:T(8,128)(2,1)S(1)} %maximum_select_fusion.refs_0_), channel_id=1, source_target_pairs={{0,16},{16,0},{1,17},{17,1},{2,18},{18,2},{3,19},{19,3},{4,20},{20... | collective-permute-start | bytes 995336 | tf_op jit(solution)/shard_map/ppermute | solution.py:223
  56.9 24.2 %collective-permute-start.5 = (bf16[288,1152]{1,0:T(8,128)(2,1)S(1)}, bf16[288,1152]{1,0:T(8,128)(2,1)S(1)}, u32[]{:S(2)}, u32[]{:S(2)}) collective-permute-start(bf16[288,1152]{1,0:T(8,128)(2,1)S(1)} %constant_dynamic-update-slice_fusion.refs_4_.refs_2_), channel_id=1, source_target_pairs={{0,16},{16,0},{1,17},{17,1},{2,18},{18,2},{3,19},{19,3},{4,20},{20... | collective-permute-start | bytes 1990664 | tf_op jit(solution)/shard_map/ppermute | solution.py:223
  56.9 23.2 %collective-permute-start.4 = (bf16[144,1152]{1,0:T(8,128)(2,1)}, bf16[144,1152]{1,0:T(8,128)(2,1)S(1)}, u32[]{:S(2)}, u32[]{:S(2)}) collective-permute-start(bf16[144,1152]{1,0:T(8,128)(2,1)} %collective-permute-done.3.refs_2_), channel_id=1, source_target_pairs={{0,16},{16,0},{1,17},{17,1},{2,18},{18,2},{3,19},{19,3},{4,20},{20... | collective-permute-start | bytes 995336 | tf_op jit(solution)/shard_map/ppermute | solution.py:223
  78.6 28.4 %collective-permute-start.17 = (bf16[432,1152]{1,0:T(8,128)(2,1)S(1)}, bf16[432,1152]{1,0:T(8,128)(2,1)S(1)}, u32[]{:S(2)}, u32[]{:S(2)}) collective-permute-start(bf16[432,1152]{1,0:T(8,128)(2,1)S(1)} %constant_dynamic-update-slice_fusion.4.refs_6_.refs_0_.refs_2_), channel_id=1, source_target_pairs={{0,1},{1,0},{2,3},{3,2},{4,5},{5,4},{6,7},{7,6},{8,9},{9,8},{10,11... | collective-permute-start | bytes 2985992 | tf_op jit(solution)/shard_map/ppermute | solution.py:223
  82.0 25.0 %collective-permute-start.16 = (bf16[288,1152]{1,0:T(8,128)(2,1)}, bf16[288,1152]{1,0:T(8,128)(2,1)}, u32[]{:S(2)}, u32[]{:S(2)}) collective-permute-start(bf16[288,1152]{1,0:T(8,128)(2,1)} %get-tuple-element.123), channel_id=1, source_target_pairs={{0,2},{1,3},{2,0},{3,1},{4,6},{5,7},{6,4},{7,5},{8,10},{9,11},{10,... | collective-permute-start | bytes 1990664 | tf_op jit(solution)/shard_map/ppermute | solution.py:223
  84.4 22.5 %collective-permute-start.15 = (bf16[144,1152]{1,0:T(8,128)(2,1)}, bf16[144,1152]{1,0:T(8,128)(2,1)S(1)}, u32[]{:S(2)}, u32[]{:S(2)}) collective-permute-start(bf16[144,1152]{1,0:T(8,128)(2,1)} %dynamic-slice_bitcast_fusion.2), channel_id=1, source_target_pairs={{0,4},{1,5},{2,6},{3,7},{4,0},{5,1},{6,2},{7,3},{8,12},{9,13},{10,... | collective-permute-start | bytes 995336 | tf_op jit(solution)/shard_map/ppermute | solution.py:223
  106.6 26.7 %collective-permute-start.13 = (bf16[448,1152]{1,0:T(8,128)(2,1)S(1)}, bf16[448,1152]{1,0:T(8,128)(2,1)S(1)}, u32[]{:S(2)}, u32[]{:S(2)}) collective-permute-start(bf16[448,1152]{1,0:T(8,128)(2,1)S(1)} %shard_map.158.refs_0_), channel_id=1, source_target_pairs={{0,8},{8,0},{1,9},{9,1},{2,10},{10,2},{3,11},{11,3},{4,12},{12,4},... | collective-permute-start | bytes 3096584 | tf_op jit(solution)/shard_map/ppermute | solution.py:223
  108.3 25.0 %collective-permute-start.22 = (bf16[432,1152]{1,0:T(8,128)(2,1)S(1)}, bf16[432,1152]{1,0:T(8,128)(2,1)S(1)}, u32[]{:S(2)}, u32[]{:S(2)}) collective-permute-start(bf16[432,1152]{1,0:T(8,128)(2,1)S(1)} %get-tuple-element.122.refs_10_.refs_4_), channel_id=1, source_target_pairs={{0,1},{1,0},{2,3},{3,2},{4,5},{5,4},{6,7},{7,6},{8,9},{9,8},{10,11... | collective-permute-start | bytes 2985992 | tf_op jit(solution)/shard_map/ppermute | solution.py:223
  108.9 23.0 %collective-permute-start.21 = (bf16[288,1152]{1,0:T(8,128)(2,1)S(1)}, bf16[288,1152]{1,0:T(8,128)(2,1)S(1)}, u32[]{:S(2)}, u32[]{:S(2)}) collective-permute-start(bf16[288,1152]{1,0:T(8,128)(2,1)S(1)} %get-tuple-element.121), channel_id=1, source_target_pairs={{0,2},{1,3},{2,0},{3,1},{4,6},{5,7},{6,4},{7,5},{8,10},{9,11},{10,... | collective-permute-start | bytes 1990664 | tf_op jit(solution)/shard_map/ppermute | solution.py:223
  110.7 23.9 %collective-permute-start.14 = (bf16[432,1152]{1,0:T(8,128)(2,1)S(1)}, bf16[432,1152]{1,0:T(8,128)(2,1)S(1)}, u32[]{:S(2)}, u32[]{:S(2)}) collective-permute-start(bf16[432,1152]{1,0:T(8,128)(2,1)S(1)} %constant_dynamic-update-slice_fusion.4.refs_6_.refs_0_.refs_2_), channel_id=1, source_target_pairs={{0,16},{16,0},{1,17},{17,1},{2,18},{18,2},{3,19},{19,3},{4,20},{20... | collective-permute-start | bytes 2985992 | tf_op jit(solution)/shard_map/ppermute | solution.py:223
  133.6 30.6 %collective-permute-start.27 = (bf16[432,1152]{1,0:T(8,128)(2,1)S(1)}, bf16[432,1152]{1,0:T(8,128)(2,1)S(1)}, u32[]{:S(2)}, u32[]{:S(2)}) collective-permute-start(bf16[432,1152]{1,0:T(8,128)(2,1)S(1)} %get-tuple-element.120.refs_8_.refs_6_), channel_id=1, source_target_pairs={{0,1},{1,0},{2,3},{3,2},{4,5},{5,4},{6,7},{7,6},{8,9},{9,8},{10,11... | collective-permute-start | bytes 2985992 | tf_op jit(solution)/shard_map/ppermute | solution.py:223
  134.6 29.6 %collective-permute-start.26 = (bf16[288,1152]{1,0:T(8,128)(2,1)S(1)}, bf16[288,1152]{1,0:T(8,128)(2,1)S(1)}, u32[]{:S(2)}, u32[]{:S(2)}) collective-permute-start(bf16[288,1152]{1,0:T(8,128)(2,1)S(1)} %get-tuple-element.119), channel_id=1, source_target_pairs={{0,2},{1,3},{2,0},{3,1},{4,6},{5,7},{6,4},{7,5},{8,10},{9,11},{10,... | collective-permute-start | bytes 1990664 | tf_op jit(solution)/shard_map/ppermute | solution.py:223
  135.7 28.4 %collective-permute-start.25 = (bf16[144,1152]{1,0:T(8,128)(2,1)S(1)}, bf16[144,1152]{1,0:T(8,128)(2,1)S(1)}, u32[]{:S(2)}, u32[]{:S(2)}) collective-permute-start(bf16[144,1152]{1,0:T(8,128)(2,1)S(1)} %copy-done.31), channel_id=1, source_target_pairs={{0,4},{1,5},{2,6},{3,7},{4,0},{5,1},{6,2},{7,3},{8,12},{9,13},{10,... | collective-permute-start | bytes 995336 | tf_op jit(solution)/shard_map/ppermute | solution.py:223
  137.8 28.5 %collective-permute-start.24 = (bf16[432,1152]{1,0:T(8,128)(2,1)S(1)}, bf16[432,1152]{1,0:T(8,128)(2,1)S(1)}, u32[]{:S(2)}, u32[]{:S(2)}) collective-permute-start(bf16[432,1152]{1,0:T(8,128)(2,1)S(1)} %get-tuple-element.120.refs_8_.refs_6_), channel_id=1, source_target_pairs={{0,16},{16,0},{1,17},{17,1},{2,18},{18,2},{3,19},{19,3},{4,20},{20... | collective-permute-start | bytes 2985992 | tf_op jit(solution)/shard_map/ppermute | solution.py:223
  165.3 37.9 %collective-permute-start.33 = (bf16[720,1152]{1,0:T(8,128)(2,1)S(1)}, bf16[720,1152]{1,0:T(8,128)(2,1)S(1)}, u32[]{:S(2)}, u32[]{:S(2)}) collective-permute-start(bf16[720,1152]{1,0:T(8,128)(2,1)S(1)} %constant_dynamic-update-slice_fusion.17.refs_10_.refs_2_), channel_id=1, source_target_pairs={{0,1},{1,0},{2,3},{3,2},{4,5},{5,4},{6,7},{7,6},{8,9},{9,8},{10,11... | collective-permute-start | bytes 4976648 | tf_op jit(solution)/shard_map/ppermute | solution.py:223
  177.1 26.1 %collective-permute-start.29 = (bf16[448,1152]{1,0:T(8,128)(2,1)}, bf16[448,1152]{1,0:T(8,128)(2,1)S(1)}, u32[]{:S(2)}, u32[]{:S(2)}) collective-permute-start(bf16[448,1152]{1,0:T(8,128)(2,1)} %shard_map.160.refs_0_), channel_id=1, source_target_pairs={{0,8},{8,0},{1,9},{9,1},{2,10},{10,2},{3,11},{11,3},{4,12},{12,4},... | collective-permute-start | bytes 3096584 | tf_op jit(solution)/shard_map/ppermute | solution.py:223
  178.3 23.2 %collective-permute-start.32 = (bf16[288,1152]{1,0:T(8,128)(2,1)S(1)}, bf16[288,1152]{1,0:T(8,128)(2,1)S(1)}, u32[]{:S(2)}, u32[]{:S(2)}) collective-permute-start(bf16[288,1152]{1,0:T(8,128)(2,1)S(1)} %get-tuple-element.115), channel_id=1, source_target_pairs={{0,2},{1,3},{2,0},{3,1},{4,6},{5,7},{6,4},{7,5},{8,10},{9,11},{10,... | collective-permute-start | bytes 1990664 | tf_op jit(solution)/shard_map/ppermute | solution.py:223
  178.6 20.7 %collective-permute-start.31 = (bf16[144,1152]{1,0:T(8,128)(2,1)S(1)}, bf16[144,1152]{1,0:T(8,128)(2,1)S(1)}, u32[]{:S(2)}, u32[]{:S(2)}) collective-permute-start(bf16[144,1152]{1,0:T(8,128)(2,1)S(1)} %dynamic-slice_bitcast_fusion), channel_id=1, source_target_pairs={{0,4},{1,5},{2,6},{3,7},{4,0},{5,1},{6,2},{7,3},{8,12},{9,13},{10,... | collective-permute-start | bytes 995336 | tf_op jit(solution)/shard_map/ppermute | solution.py:223
  180.2 25.5 %collective-permute-start.30 = (bf16[720,1152]{1,0:T(8,128)(2,1)S(1)}, bf16[720,1152]{1,0:T(8,128)(2,1)S(1)}, u32[]{:S(2)}, u32[]{:S(2)}) collective-permute-start(bf16[720,1152]{1,0:T(8,128)(2,1)S(1)} %constant_dynamic-update-slice_fusion.17.refs_10_.refs_2_), channel_id=1, source_target_pairs={{0,16},{16,0},{1,17},{17,1},{2,18},{18,2},{3,19},{19,3},{4,20},{20... | collective-permute-start | bytes 4976648 | tf_op jit(solution)/shard_map/ppermute | solution.py:223
  204.2 24.5 %collective-permute-start.38 = (bf16[432,1152]{1,0:T(8,128)(2,1)S(1)}, bf16[432,1152]{1,0:T(8,128)(2,1)}, u32[]{:S(2)}, u32[]{:S(2)}) collective-permute-start(bf16[432,1152]{1,0:T(8,128)(2,1)S(1)} %get-tuple-element.114.refs_6_.refs_14_), channel_id=1, source_target_pairs={{0,1},{1,0},{2,3},{3,2},{4,5},{5,4},{6,7},{7,6},{8,9},{9,8},{10,11... | collective-permute-start | bytes 2985992 | tf_op jit(solution)/shard_map/ppermute | solution.py:223
  205.3 23.5 %collective-permute-start.37 = (bf16[288,1152]{1,0:T(8,128)(2,1)S(1)}, bf16[288,1152]{1,0:T(8,128)(2,1)}, u32[]{:S(2)}, u32[]{:S(2)}) collective-permute-start(bf16[288,1152]{1,0:T(8,128)(2,1)S(1)} %get-tuple-element.113), channel_id=1, source_target_pairs={{0,2},{1,3},{2,0},{3,1},{4,6},{5,7},{6,4},{7,5},{8,10},{9,11},{10,... | collective-permute-start | bytes 1990664 | tf_op jit(solution)/shard_map/ppermute | solution.py:223
  229.8 24.0 %collective-permute-start.35 = (bf16[448,1152]{1,0:T(8,128)(2,1)}, bf16[448,1152]{1,0:T(8,128)(2,1)}, u32[]{:S(2)}, u32[]{:S(2)}) collective-permute-start(bf16[448,1152]{1,0:T(8,128)(2,1)} %get-tuple-element.85.refs_0_), channel_id=1, source_target_pairs={{0,8},{8,0},{1,9},{9,1},{2,10},{10,2},{3,11},{11,3},{4,12},{12,4},... | collective-permute-start | bytes 3096584 | tf_op jit(solution)/shard_map/ppermute | solution.py:223
  (65 other events, 690.8 us)
